TPU v7x, 512 devices: a whole 4x4x16 slice. The times are simulated.
512 devices in a mesh: patch: 64 (over x, z_hi, y, core), uly: 8 (over z_lo).
Axes of the slice: x: 4, y: 4, z: 16 (z_hi: 2, z_lo: 8; z = z_hi * 8 + z_lo), core: 2. Of those that a mesh axis runs over, the one named last changes fastest.
Arguments:
- queries: bfloat16 [8192, 3072], P(('patch', 'uly')), may hold values from -512 to 512
- keys_new: bfloat16 [8192, 3072], P(('patch', 'uly')), may hold values from -6 to 6
- values_new: bfloat16 [8192, 3072], P(('patch', 'uly')), may hold values from -6 to 6
- keys_old: bfloat16 [8192, 3072], P(('patch', 'uly')), may hold values from -8 to 8
- values_old: bfloat16 [8192, 3072], P(('patch', 'uly')), may hold values from -6 to 6
- gate_table: float32 [50, 3072], replicated, may hold values from 0.5 to 2
- step_index: int32 [1], replicated, may hold values from 0 to 49
Outputs:
- attended: bfloat16 [8192, 3072], P(('patch', 'uly'))
All inputs are finite; a program needn't handle non-finite values.
Results may differ from a plain program's by a relative error of at most 0.0045.
Values may be sent and summed in bfloat16 or wider, within the bound.
A program may use at most 64 MiB of HBM per device.

v0:
```python
import jax
import jax.numpy as jnp
from jax import lax
from jax.sharding import PartitionSpec as P

HEADS = 24
HEAD_DIM = 128


def sent_together(arrays, axis, dim, along):
    both = jnp.concatenate(arrays, axis=along)
    result, at, outs = (lax.all_gather(both, axis, axis=dim, tiled=True), 0, [])
    for a in arrays:
        outs.append(lax.slice_in_dim(result, at, at + a.shape[along], axis=along))
        at += a.shape[along]
    return tuple(outs)


def absorb(carry, query_heads, key_piece, value_piece, masked):
    run_max, run_total, accumulated = carry
    score = jnp.einsum(
        "phd,khd->hpk", query_heads, key_piece, preferred_element_type=jnp.float32
    ) * HEAD_DIM ** (-0.5)
    score = jnp.where(masked[None, None, :], jnp.float32(-1e30), score)
    new_max = jnp.maximum(run_max, jnp.max(score, axis=-1))
    shrink = jnp.exp(run_max - new_max)
    expo = jnp.exp(score - new_max[..., None])
    run_total = run_total * shrink + jnp.sum(expo, axis=-1)
    update = jnp.einsum(
        "hpk,khd->phd", expo.astype(jnp.bfloat16), value_piece, preferred_element_type=jnp.float32
    )
    accumulated = accumulated * jnp.transpose(shrink)[..., None] + update
    return (new_max, run_total, accumulated)


def absorb_blocks(carry, query_heads, key_piece, value_piece, masked):
    count = key_piece.shape[0]
    span = 2048
    heads_here = key_piece.shape[1]
    key_blocks = key_piece.reshape(count // span, span, heads_here, HEAD_DIM)
    value_blocks = value_piece.reshape(count // span, span, heads_here, HEAD_DIM)
    mask_blocks = masked.reshape(count // span, span)

    def one_block(state, pieces):
        return (absorb(state, query_heads, pieces[0], pieces[1], pieces[2]), None)

    carry, unused = lax.scan(one_block, carry, (key_blocks, value_blocks, mask_blocks))
    return carry


def body(queries, keys_new, values_new, keys_old, values_old, gate_table, step_index):
    groups = lax.axis_size("uly")
    heads_here = HEADS // groups
    width_here = heads_here * HEAD_DIM
    patch_here = lax.axis_index("patch")
    fresh = (
        lax.all_to_all(queries, "uly", split_axis=1, concat_axis=0, tiled=True),
        lax.all_to_all(keys_new, "uly", split_axis=1, concat_axis=0, tiled=True),
        lax.all_to_all(values_new, "uly", split_axis=1, concat_axis=0, tiled=True),
    )
    query_heads = fresh[0].reshape(-1, heads_here, HEAD_DIM)
    fresh_keys = fresh[1].reshape(-1, heads_here, HEAD_DIM)
    fresh_values = fresh[2].reshape(-1, heads_here, HEAD_DIM)
    patch_rows = query_heads.shape[0]
    score = jnp.einsum(
        "phd,khd->hpk", query_heads, fresh_keys, preferred_element_type=jnp.float32
    ) * HEAD_DIM ** (-0.5)
    run_max = jnp.max(score, axis=-1)
    expo = jnp.exp(score - run_max[..., None])
    run_total = jnp.sum(expo, axis=-1)
    accumulated = jnp.einsum(
        "hpk,khd->phd", expo.astype(jnp.bfloat16), fresh_values, preferred_element_type=jnp.float32
    )
    carry = (run_max, run_total, accumulated)
    stale = (
        lax.all_to_all(keys_old, "uly", split_axis=1, concat_axis=0, tiled=True),
        lax.all_to_all(values_old, "uly", split_axis=1, concat_axis=0, tiled=True),
    )
    stale_keys = stale[0].reshape(-1, heads_here, HEAD_DIM)
    stale_values = stale[1].reshape(-1, heads_here, HEAD_DIM)
    pieces = sent_together((stale_keys, stale_values), "patch", 0, 1)
    count = pieces[0].shape[0]
    masked = jnp.arange(count, dtype=jnp.int32) // patch_rows == patch_here
    carry = absorb_blocks(carry, query_heads, pieces[0], pieces[1], masked)
    run_max, run_total, accumulated = carry
    picker = (jnp.arange(gate_table.shape[0], dtype=jnp.int32) == step_index[0]).astype(jnp.float32)
    gate = jnp.dot(picker, gate_table, precision=lax.Precision.HIGHEST)
    gate_here = lax.dynamic_slice_in_dim(gate, lax.axis_index("uly") * width_here, width_here, 0)
    mixed = (accumulated / jnp.transpose(run_total)[..., None]).reshape(patch_rows, width_here)
    gated = (mixed * gate_here).astype(jnp.bfloat16)
    return lax.all_to_all(gated, "uly", split_axis=0, concat_axis=1, tiled=True)


def solution(mesh):
    in_specs = (
        P(("patch", "uly"), None),
        P(("patch", "uly"), None),
        P(("patch", "uly"), None),
        P(("patch", "uly"), None),
        P(("patch", "uly"), None),
        P(),
        P(),
    )
    out_specs = P(("patch", "uly"), None)
    return jax.shard_map(body, mesh=mesh, in_specs=in_specs, out_specs=out_specs, check_vma=False)
```

profile of v0, /device:TPU:1, one launch (start us, length us, event | category | flops | bytes accessed | tf_op | source)
XLA Modules:
  0.0 313.7 jit_solution(12219189061899668328)
XLA Ops:
  6.5 0.0 copy-start
  6.5 0.0 copy-start.1
  6.5 1.6 copy.86
  8.1 13.1 %all-to-all-start.3 = ((bf16[16,8,384]{2,0,1:T(8,128)(2,1)}), bf16[16,8,384]{2,0,1:T(8,128)(2,1)S(1)}, u32[]{:S(2)}, u32[]{:S(2)}) async-start(bf16[16,8,384]{2,0,1:T(8,128)(2,1)} %bitcast.72), calls=%async_computation.3 | async-start | bytes 196608 | tf_op jit(solution)/shard_map/all_to_all | solution.py:76
  21.2 1.5 copy.85
  22.8 8.5 %all-to-all-done.3 = bf16[16,8,384]{2,0,1:T(8,128)(2,1)S(1)} async-done(((bf16[16,8,384]{2,0,1:T(8,128)(2,1)}), bf16[16,8,384]{2,0,1:T(8,128)(2,1)S(1)}, u32[]{:S(2)}, u32[]{:S(2)}) %all-to-all-start.3) | async-done | bytes 98336 | tf_op jit(solution)/shard_map/all_to_all | solution.py:76
  31.3 4.6 %all-to-all-start.4 = ((bf16[16,8,384]{2,0,1:T(8,128)(2,1)}), bf16[16,8,384]{2,0,1:T(8,128)(2,1)S(1)}, u32[]{:S(2)}, u32[]{:S(2)}) async-start(bf16[16,8,384]{2,0,1:T(8,128)(2,1)} %bitcast.71), calls=%async_computation.4 | async-start | bytes 196608 | tf_op jit(solution)/shard_map/all_to_all | solution.py:77
  35.8 0.0 all-gather.2.cloned.1.call-start
  35.9 9.9 %all-to-all-done.4 = bf16[16,8,384]{2,0,1:T(8,128)(2,1)S(1)} async-done(((bf16[16,8,384]{2,0,1:T(8,128)(2,1)}), bf16[16,8,384]{2,0,1:T(8,128)(2,1)S(1)}, u32[]{:S(2)}, u32[]{:S(2)}) %all-to-all-start.4) | async-done | bytes 98336 | tf_op jit(solution)/shard_map/all_to_all | solution.py:77
  45.9 0.1 pad_maximum_fusion
  46.0 0.7 copy.57
  46.7 0.0 all-gather.2.cloned.1.call-update
  46.8 1.5 copy.89
  48.3 4.6 %all-to-all-start = ((bf16[16,8,384]{2,0,1:T(8,128)(2,1)}), bf16[16,8,384]{2,0,1:T(8,128)(2,1)S(1)}, u32[]{:S(2)}, u32[]{:S(2)}) async-start(bf16[16,8,384]{2,0,1:T(8,128)(2,1)} %bitcast.75), calls=%async_computation | async-start | bytes 196608 | tf_op jit(solution)/shard_map/all_to_all | solution.py:57
  52.9 1.5 copy.88
  54.4 8.5 %all-to-all-done = bf16[16,8,384]{2,0,1:T(8,128)(2,1)S(1)} async-done(((bf16[16,8,384]{2,0,1:T(8,128)(2,1)}), bf16[16,8,384]{2,0,1:T(8,128)(2,1)S(1)}, u32[]{:S(2)}, u32[]{:S(2)}) %all-to-all-start) | async-done | bytes 98336 | tf_op jit(solution)/shard_map/all_to_all | solution.py:57
  62.9 4.6 %all-to-all-start.1 = ((bf16[16,8,384]{2,0,1:T(8,128)(2,1)}), bf16[16,8,384]{2,0,1:T(8,128)(2,1)S(1)}, u32[]{:S(2)}, u32[]{:S(2)}) async-start(bf16[16,8,384]{2,0,1:T(8,128)(2,1)} %bitcast.74), calls=%async_computation.1 | async-start | bytes 196608 | tf_op jit(solution)/shard_map/all_to_all | solution.py:58
  67.5 0.0 copy-done.1
  67.5 0.7 copy.87
  68.8 12.8 %all-to-all-done.1 = bf16[16,8,384]{2,0,1:T(8,128)(2,1)S(1)} async-done(((bf16[16,8,384]{2,0,1:T(8,128)(2,1)}), bf16[16,8,384]{2,0,1:T(8,128)(2,1)S(1)}, u32[]{:S(2)}, u32[]{:S(2)}) %all-to-all-start.1) | async-done | bytes 98336 | tf_op jit(solution)/shard_map/all_to_all | solution.py:58
  81.6 3.6 %all-to-all-start.2 = ((bf16[16,8,384]{2,0,1:T(8,128)(2,1)}), bf16[16,8,384]{2,0,1:T(8,128)(2,1)S(1)}, u32[]{:S(2)}, u32[]{:S(2)}) async-start(bf16[16,8,384]{2,0,1:T(8,128)(2,1)} %bitcast.73), calls=%async_computation.2 | async-start | bytes 196608 | tf_op jit(solution)/shard_map/all_to_all | solution.py:59
  85.1 0.0 copy-done
  85.2 0.3 fusion.33
  85.5 0.1 dynamic_slice.14
  85.6 0.1 fusion.30
  85.7 9.4 %all-to-all-done.2 = bf16[16,8,384]{2,0,1:T(8,128)(2,1)S(1)} async-done(((bf16[16,8,384]{2,0,1:T(8,128)(2,1)}), bf16[16,8,384]{2,0,1:T(8,128)(2,1)S(1)}, u32[]{:S(2)}, u32[]{:S(2)}) %all-to-all-start.2) | async-done | bytes 98336 | tf_op jit(solution)/shard_map/all_to_all | solution.py:59
  95.2 0.2 fusion.39
  95.4 0.2 convolution_bitcast_fusion
  95.7 0.1 copy.58
  95.8 0.1 fusion.24
  95.8 167.8 %all-gather.2.cloned.1.call-done = bf16[8192,6,128]{2,0,1:T(8,128)(2,1)} async-done(((bf16[128,6,128]{2,0,1:T(8,128)(2,1)}), bf16[8192,6,128]{2,0,1:T(8,128)(2,1)}) %all-gather.2.cloned.1.call-update) | async-done | bytes 12582928 | tf_op jit(solution)/shard_map/all_gather | solution.py:12
  263.6 10.1 %fusion.38 = (bf16[8192,3,128]{2,0,1:T(8,128)(2,1)}, bf16[8192,3,128]{2,0,1:T(8,128)(2,1)}) fusion(bf16[8192,6,128]{2,0,1:T(8,128)(2,1)} %all-gather.2.cloned.1.call-done), kind=kLoop, calls=%fused_computation.51 | loop fusion | bytes 25165824 | tf_op jit(solution)/shard_map/slice | solution.py:14
  273.7 19.6 %while.14 = (s32[]{:T(128)}, f32[3,128]{1,0:T(4,128)S(1)}, f32[3,128]{1,0:T(4,128)S(1)}, f32[128,3,128]{0,2,1:T(8,128)S(1)}, pred[4,2048]{1,0:T(4,128)(4,1)S(1)}...) while((s32[]{:T(128)}, f32[3,128]{1,0:T(4,128)S(1)}, ...), condition=%wide.region_5.6_spmd, body=%wide.region_2.5_spmd.sunk | while | flops 408257664 | bytes 13106273 | solution.py:47
  273.7 2.0 bitcast_reduce_fusion.2
  275.8 2.4 fusion.54
  278.1 0.4 fusion.53
  278.6 2.0 bitcast_reduce_fusion.2
  280.7 2.4 fusion.54
  283.0 0.4 fusion.53
  283.5 2.0 bitcast_reduce_fusion.2
  285.6 2.4 fusion.54
  287.9 0.4 fusion.53
  288.5 2.0 bitcast_reduce_fusion.2
  290.5 2.4 fusion.54
  292.9 0.4 fusion.53
  293.4 0.1 copy.62
  293.5 0.1 reshape.75
  293.7 12.5 %all_to_all.96 = bf16[8,16,384]{2,1,0:T(8,128)(2,1)S(1)} all-to-all(bf16[8,16,384]{2,1,0:T(8,128)(2,1)S(1)} %multiply_convert_fusion), channel_id=1, replica_groups=mesh['patch'=64,'uly'=8] {'uly'}, dimensions={0} | all-to-all | bytes 196608 | tf_op jit(solution)/shard_map/all_to_all | solution.py:91
  306.2 0.7 copy.73
  (24 shorter events, 0.5 us)
Async XLA Ops:
  6.5 78.6 %copy-start = (f32[50,3072]{1,0:T(8,128)S(1)}, f32[50,3072]{1,0:T(8,128)}, u32[]{:S(2)}) copy-start(f32[50,3072]{1,0:T(8,128)} %param.14) | copy-start | bytes 1843204
  6.5 60.9 %copy-start.1 = (bf16[16,3072]{1,0:T(8,128)(2,1)S(1)}, bf16[16,3072]{1,0:T(8,128)(2,1)}, u32[]{:S(2)}) copy-start(bf16[16,3072]{1,0:T(8,128)(2,1)} %param.11) | copy-start | bytes 294916
  8.1 23.1 %all-to-all-start.3 = ((bf16[16,8,384]{2,0,1:T(8,128)(2,1)}), bf16[16,8,384]{2,0,1:T(8,128)(2,1)S(1)}, u32[]{:S(2)}, u32[]{:S(2)}) async-start(bf16[16,8,384]{2,0,1:T(8,128)(2,1)} %bitcast.72), calls=%async_computation.3 | async-start | bytes 196608 | tf_op jit(solution)/shard_map/all_to_all | solution.py:76
  31.3 14.6 %all-to-all-start.4 = ((bf16[16,8,384]{2,0,1:T(8,128)(2,1)}), bf16[16,8,384]{2,0,1:T(8,128)(2,1)S(1)}, u32[]{:S(2)}, u32[]{:S(2)}) async-start(bf16[16,8,384]{2,0,1:T(8,128)(2,1)} %bitcast.71), calls=%async_computation.4 | async-start | bytes 196608 | tf_op jit(solution)/shard_map/all_to_all | solution.py:77
  35.8 227.8 %all-gather.2.cloned.1.call-start = ((), (), s32[]{:S(2)}) async-start(), calls=%async_computation.6 | async-start | bytes 12779520 | tf_op jit(solution)/shard_map/all_gather | solution.py:12
  48.3 14.6 %all-to-all-start = ((bf16[16,8,384]{2,0,1:T(8,128)(2,1)}), bf16[16,8,384]{2,0,1:T(8,128)(2,1)S(1)}, u32[]{:S(2)}, u32[]{:S(2)}) async-start(bf16[16,8,384]{2,0,1:T(8,128)(2,1)} %bitcast.75), calls=%async_computation | async-start | bytes 196608 | tf_op jit(solution)/shard_map/all_to_all | solution.py:57
  62.9 18.7 %all-to-all-start.1 = ((bf16[16,8,384]{2,0,1:T(8,128)(2,1)}), bf16[16,8,384]{2,0,1:T(8,128)(2,1)S(1)}, u32[]{:S(2)}, u32[]{:S(2)}) async-start(bf16[16,8,384]{2,0,1:T(8,128)(2,1)} %bitcast.74), calls=%async_computation.1 | async-start | bytes 196608 | tf_op jit(solution)/shard_map/all_to_all | solution.py:58
  81.6 13.6 %all-to-all-start.2 = ((bf16[16,8,384]{2,0,1:T(8,128)(2,1)}), bf16[16,8,384]{2,0,1:T(8,128)(2,1)S(1)}, u32[]{:S(2)}, u32[]{:S(2)}) async-start(bf16[16,8,384]{2,0,1:T(8,128)(2,1)} %bitcast.73), calls=%async_computation.2 | async-start | bytes 196608 | tf_op jit(solution)/shard_map/all_to_all | solution.py:59
Sparse Core Ops, SparseCore 0:
  46.9 216.6 all-gather.1
where the time goes:
time: 315 us; the launch traced here: 314 us
  waiting for transfers between devices  217 us (69%)
  starting transfers between devices  30.4 us (10%)
  local copies, waits for them, and re-layouts  19.1 us (6%)
  matrix products  18.3 us (6%)
  between operations  14.1 us (4%)
  blocking collectives  12.5 us (4%)
    all_gather x1, waiting for transfers between devices, sent_together(): result, at, outs = (lax.all_gather(both, axis, axis=dim, tiled=True), 0, [])  168 us
    all_to_all x1, starting transfers between devices, body(): lax.all_to_all(keys_old, 'uly', split_axis=1, concat_axis=0, tiled=True)  13.1 us
    all_to_all x1, waiting for transfers between devices, body(): lax.all_to_all(keys_new, 'uly', split_axis=1, concat_axis=0, tiled=True)  12.8 us
    all_to_all x1, blocking collectives, body(): return lax.all_to_all(gated, 'uly', split_axis=0, concat_axis=1, tiled=True)  12.5 us
    slice x1, local copies, waits for them, and re-layouts, sent_together(): outs.append(lax.slice_in_dim(result, at, at + a.shape[along], axis=along))  10.1 us
    all_to_all x1, waiting for transfers between devices, body(): lax.all_to_all(values_old, 'uly', split_axis=1, concat_axis=0, tiled=True)  9.93 us
    all_to_all x1, waiting for transfers between devices, body(): lax.all_to_all(values_new, 'uly', split_axis=1, concat_axis=0, tiled=True)  9.43 us
    dot_general x4, matrix products, absorb(): jnp.einsum('hpk,khd->phd', expo.astype(jnp.bfloat16), value_piece, prefer...  9.42 us
  transfers between devices with their start and end apart: 6, of which 6 were waited for; matrix products, arithmetic and copies ran while one was open for 2% of the time, Pallas kernels for 0%

commit v1 on v0

v1 whole, which is shorter than its diff:
```python
import jax
import jax.numpy as jnp
from jax import lax
from jax.experimental import pallas as pl
from jax.experimental.pallas import tpu as pltpu
from jax.sharding import PartitionSpec as P

HEADS = 24
HEAD_DIM = 128
MESH = pl.DeviceIdType.MESH
TOK = 16
RING = 16
SIDE = 4
C = HEAD_DIM ** (-0.5) * 1.4426950408889634

ORDER = (
    (0, 0), (1, 0), (3, 0), (0, 1), (0, 3), (2, 0), (1, 1), (1, 3),
    (3, 1), (3, 3), (0, 2), (2, 1), (2, 3), (1, 2), (3, 2), (2, 2),
)
SLOT = {pair: at for at, pair in enumerate(ORDER)}
OWN_STEP = 8


def kernel(
    q_in, kn_in, vn_in, ko_in, vo_in, gate_in, step_ref, out_ref,
    stage, gbuf, kv, qa, acc, mx, tot, stat, racc, rstat, obuf, outbuf,
    stage_sem, gate_sem, kv_send, kv_recv, q_send, q_recv, qf_send, qf_recv,
    new_send, new_recv, old_sem, xy_send, xy_recv, part_send, part_recv, out_send, out_recv,
):
    p = lax.axis_index("patch")
    zl = lax.axis_index("uly")
    c = lax.rem(p, 2)
    y = lax.rem(p // 2, SIDE)
    zh = lax.rem(p // 8, 2)
    x = p // 16
    z = zh * 8 + zl
    g, s = z // 2, lax.rem(z, 2)

    def patch_of(x_, zh_, y_, c_):
        return ((x_ * 2 + zh_) * SIDE + y_) * 2 + c_

    def z_dev(z_):
        return {"patch": patch_of(x, z_ // 8, y, c), "uly": lax.rem(z_, 8)}

    def xy_dev(da, db):
        x_ = lax.rem(x + da * (1 - c) + db * c, SIDE)
        y_ = lax.rem(y + da * c + db * (1 - c), SIDE)
        return {"patch": patch_of(x_, zh, y_, c), "uly": zl}

    partner = {"patch": patch_of(x, zh, y, 1 - c), "uly": zl}

    def lanes(at, n=HEAD_DIM):
        return pl.ds(pl.multiple_of(at, HEAD_DIM), n)

    def rows(at, n):
        return pl.ds(pl.multiple_of(at, TOK), n)

    def remote(src, dst, ssem, rsem, dev):
        return pltpu.make_async_remote_copy(
            src_ref=src, dst_ref=dst, send_sem=ssem, recv_sem=rsem, device_id=dev, device_id_type=MESH
        )

    col = lanes((3 * g + s) * HEAD_DIM, 256)
    loads = [
        pltpu.make_async_copy(ref, stage.at[at], stage_sem.at[at])
        for at, ref in enumerate((ko_in, vo_in, q_in, kn_in, vn_in))
    ]
    for load in loads:
        load.start()
    gate_load = pltpu.make_async_copy(gate_in.at[:, col], gbuf, gate_sem)
    gate_load.start()

    barrier = pltpu.get_barrier_semaphore()

    def greet(d, carry):
        pl.semaphore_signal(barrier, inc=1, device_id=z_dev(lax.rem(z + d, RING)), device_id_type=MESH)
        return carry

    lax.fori_loop(1, RING, greet, 0)
    for da, db in ((1, 0), (3, 0), (0, 1), (0, 3)):
        pl.semaphore_signal(barrier, inc=1, device_id=xy_dev(da, db), device_id_type=MESH)
    pl.semaphore_signal(barrier, inc=1, device_id=partner, device_id_type=MESH)
    acc[...] = jnp.zeros_like(acc)
    tot[...] = jnp.zeros_like(tot)
    mx[...] = jnp.full_like(mx, -1e30)
    for load in loads:
        load.wait()
    pl.semaphore_wait(barrier, RING - 1 + 4 + 1)

    mine = rows(z * TOK, TOK)
    here = rows(zl * TOK, TOK)

    def far(i):
        return lax.rem(z + 8 + ((i + 1) // 2) * (2 * lax.rem(i, 2) - 1), RING)

    def two_heads(z_):
        return lanes((3 * (z_ // 2) + lax.rem(z_, 2)) * HEAD_DIM, 256)

    def main_head(z_):
        return lanes((3 * (z_ // 2) + 2 * lax.rem(z_, 2)) * HEAD_DIM)

    def send_kv(i, carry):
        t = far(i)
        for at in range(2):
            remote(
                stage.at[at, :, two_heads(t)], kv.at[0, mine, 256 * at:256 * at + 256],
                kv_send, kv_recv, z_dev(t),
            ).start()
        return carry

    lax.fori_loop(0, RING - 1, send_kv, 0)
    for at in range(2):
        pltpu.make_async_copy(
            stage.at[at, :, two_heads(z)], kv.at[0, mine, 256 * at:256 * at + 256], kv_recv
        ).start()

    def send_q(i, carry):
        t = far(i)

        @pl.when(lax.rem(t, 2) == zh)
        def _():
            remote(stage.at[2, :, two_heads(t)], qa.at[c, mine, :], q_send, q_recv, z_dev(t)).start()

        @pl.when(lax.rem(t, 2) != zh)
        def _():
            remote(
                stage.at[2, :, main_head(t)], qa.at[c, mine, lanes(lax.rem(t, 2) * HEAD_DIM)],
                q_send, q_recv, z_dev(t),
            ).start()

        return carry

    lax.fori_loop(0, RING - 1, send_q, 0)

    def send_new(i, carry):
        t = far(i)

        @pl.when(lax.rem(t, 2) == zh)
        def _():
            for at in range(2):
                remote(
                    stage.at[3 + at, :, two_heads(t)], kv.at[RING + zh, mine, 256 * at:256 * at + 256],
                    new_send, new_recv, z_dev(t),
                ).start()

        @pl.when(lax.rem(t, 2) != zh)
        def _():
            for at in range(2):
                remote(
                    stage.at[3 + at, :, main_head(t)],
                    kv.at[RING + zh, mine, lanes(256 * at + lax.rem(t, 2) * HEAD_DIM)],
                    new_send, new_recv, z_dev(t),
                ).start()

        return carry

    lax.fori_loop(0, RING - 1, send_new, 0)

    @pl.when(s == zh)
    def _():
        pltpu.make_async_copy(stage.at[2, :, two_heads(z)], qa.at[c, mine, :], q_recv).start()
        for at in range(2):
            pltpu.make_async_copy(
                stage.at[3 + at, :, two_heads(z)], kv.at[RING + zh, mine, 256 * at:256 * at + 256], new_recv
            ).start()

    @pl.when(s != zh)
    def _():
        pltpu.make_async_copy(
            stage.at[2, :, main_head(z)], qa.at[c, mine, lanes(s * HEAD_DIM)], q_recv
        ).start()
        for at in range(2):
            pltpu.make_async_copy(
                stage.at[3 + at, :, main_head(z)],
                kv.at[RING + zh, mine, lanes(256 * at + s * HEAD_DIM)], new_recv,
            ).start()

    half_rows = (slice(0, 128), slice(128, 256))

    def push(src, dst, da, db, part=None):
        a, b = kv.at[SLOT[src]], kv.at[SLOT[dst]]
        if part is not None:
            a, b = kv.at[SLOT[src], half_rows[part]], kv.at[SLOT[dst], half_rows[part]]
        remote(a, b, xy_send, xy_recv.at[SLOT[dst]], xy_dev(da, db)).start()

    def pass_on(pair):
        da, db = pair
        if pair == (0, 0):
            push(pair, (1, 0), 1, 0)
            push(pair, (3, 0), 3, 0)
        if pair == (1, 0):
            push(pair, (2, 0), 1, 0, 0)
        if pair == (3, 0):
            push(pair, (2, 0), 3, 0, 1)
        if db == 0:
            push(pair, (da, 1), 0, 1)
            push(pair, (da, 3), 0, 3)
        if db == 1:
            push(pair, (da, 2), 0, 1, 0)
        if db == 3:
            push(pair, (da, 2), 0, 3, 1)

    pltpu.make_async_copy(kv.at[0], kv.at[0], kv_recv).wait()
    pass_on((0, 0))
    for side in range(2):
        keep = half_rows[1 - side]
        pltpu.make_async_copy(kv.at[0, keep], kv.at[RING + side, keep], old_sem.at[side]).start()

    pltpu.make_async_copy(qa.at[c, 0:192], qa.at[c, 0:192], q_recv).wait()
    main_col, shared_col = lanes(s * HEAD_DIM), lanes((1 - s) * HEAD_DIM)
    shared_rows = rows(s * 128, 128)
    q_main = remote(
        qa.at[c, :, main_col], qa.at[c, :, main_col], qf_send.at[0], qf_recv.at[0], partner
    )
    q_shared = remote(
        qa.at[c, shared_rows, shared_col], qa.at[c, shared_rows, shared_col],
        qf_send.at[1], qf_recv.at[1], partner,
    )
    q_main.start()
    q_shared.start()
    q_main.wait()
    q_shared.wait()

    def absorb(core, at, count, queries, keys, values):
        dots = lax.dot_general(queries, keys, (((1,), (1,)), ((), ())), preferred_element_type=jnp.float32)
        there = (core, pl.ds(at, count))
        old = mx[there]
        new = jnp.maximum(old, jnp.max(dots, axis=1, keepdims=True))
        shrink = jnp.exp2((old - new) * C)
        expo = jnp.exp2((dots - new[:, :1]) * C)
        tot[there] = tot[there] * shrink + jnp.sum(expo, axis=1, keepdims=True)
        acc[there] = acc[there] * shrink + jnp.dot(
            expo.astype(jnp.bfloat16), values, preferred_element_type=jnp.float32
        )
        mx[there] = new

    main_val, shared_val = lanes(256 + s * HEAD_DIM), lanes(256 + (1 - s) * HEAD_DIM)

    def chunk(core, at):
        absorb(core, 0, 256, qa[core, :, main_col], kv[at, :, main_col], kv[at, :, main_val])
        absorb(
            core, 256, 128, qa[core, shared_rows, shared_col], kv[at, :, shared_col], kv[at, :, shared_val]
        )

    def own():
        pltpu.make_async_copy(kv.at[RING, 0:192], kv.at[RING, 0:192], new_recv).wait()
        for side in range(2):
            keep = half_rows[1 - side]
            pltpu.make_async_copy(kv.at[0, keep], kv.at[RING + side, keep], old_sem.at[side]).wait()
        chunk(1 - c, 0)
        for side in range(2):
            at = RING + side
            absorb(
                c, side * 128, 128, qa[c, half_rows[side], main_col], kv[at, :, main_col], kv[at, :, main_val]
            )
        at = RING + s
        absorb(c, 256, 128, qa[c, shared_rows, shared_col], kv[at, :, shared_col], kv[at, :, shared_val])

    partial = [
        remote(acc.at[1 - c], racc, part_send.at[0], part_recv.at[0], partner),
        remote(stat, rstat, part_send.at[1], part_recv.at[1], partner),
    ]

    def one_slot(k, carry):
        pltpu.make_async_copy(kv.at[k], kv.at[k], xy_recv.at[k]).wait()
        for at, pair in enumerate(ORDER):
            if at > 0 and pair[1] != 2:
                @pl.when(k == at)
                def _(pair=pair):
                    pass_on(pair)

        @pl.when(k == OWN_STEP)
        def _():
            own()

        chunk(1 - c, k)

        @pl.when(k == RING - 1)
        def _():
            low = lax.broadcasted_iota(jnp.int32, stat.shape, 1) < 64
            stat[...] = jnp.where(low, mx[1 - c], tot[1 - c])
            for copy in partial:
                copy.start()

        chunk(c, k)
        return carry

    lax.fori_loop(1, RING, one_slot, 0)

    gate_load.wait()
    picked = lax.broadcasted_iota(jnp.int32, gbuf.shape, 0) == step_ref[0]
    gate = jnp.sum(jnp.where(picked, gbuf[...], 0.0), axis=0, keepdims=True)
    gate_lo, gate_hi = gate[:, :HEAD_DIM], gate[:, HEAD_DIM:]
    gate_main = jnp.where(s == 0, gate_lo, gate_hi)
    gate_shared = jnp.where(s == 0, gate_hi, gate_lo)
    for copy in partial:
        copy.wait()
    for at, count, gated in ((0, 256, gate_main), (256, 128, gate_shared)):
        there = pl.ds(at, count)
        m1, m2 = mx[c, there], jnp.broadcast_to(rstat[there, 0:1], (count, HEAD_DIM))
        l2 = jnp.broadcast_to(rstat[there, 64:65], (count, HEAD_DIM))
        top = jnp.maximum(m1, m2)
        w1, w2 = jnp.exp2((m1 - top) * C), jnp.exp2((m2 - top) * C)
        mixed = (acc[c, there] * w1 + racc[there] * w2) / (tot[c, there] * w1 + l2 * w2)
        obuf[there] = (mixed * gated).astype(jnp.bfloat16)

    my_main, my_shared = main_head(z), lanes((3 * g + 1) * HEAD_DIM)

    def send_out(i, carry):
        t = far(i)
        remote(obuf.at[rows(t * TOK, TOK)], outbuf.at[:, my_main], out_send, out_recv, z_dev(t)).start()

        @pl.when(t // 8 == s)
        def _():
            remote(
                obuf.at[rows(256 + lax.rem(t, 8) * TOK, TOK)], outbuf.at[:, my_shared],
                out_send, out_recv, z_dev(t),
            ).start()

        return carry

    lax.fori_loop(0, RING - 1, send_out, 0)
    pltpu.make_async_copy(obuf.at[mine], outbuf.at[:, my_main], out_recv).start()

    @pl.when(zh == s)
    def _():
        pltpu.make_async_copy(
            obuf.at[rows(256 + zl * TOK, TOK)], outbuf.at[:, my_shared], out_recv
        ).start()

    def sent(ref, sem):
        pltpu.make_async_copy(ref, ref, sem).wait()

    sent(kv.at[0, 0:240], kv_send)
    sent(kv.at[pl.ds(1, 15)], xy_send)

    @pl.when(zh == s)
    def _():
        sent(qa.at[0, 0:176], q_send)
        sent(kv.at[RING, 0:176], new_send)
        sent(obuf.at[pl.ds(0, 22 * TOK)], out_send)

    @pl.when(zh != s)
    def _():
        sent(qa.at[0, 0:184], q_send)
        sent(kv.at[RING, 0:184], new_send)
        sent(obuf.at[pl.ds(0, 23 * TOK)], out_send)

    pltpu.make_async_copy(outbuf, outbuf, out_recv).wait()
    out_ref[...] = outbuf[...]


def body(queries, keys_new, values_new, keys_old, values_old, gate_table, step_index):
    bf, f32 = jnp.bfloat16, jnp.float32
    dma = pltpu.SemaphoreType.DMA
    return pl.pallas_call(
        kernel,
        out_shape=jax.ShapeDtypeStruct(queries.shape, bf),
        in_specs=[pl.BlockSpec(memory_space=pl.ANY)] * 6 + [pl.BlockSpec(memory_space=pltpu.SMEM)],
        out_specs=pl.BlockSpec(memory_space=pltpu.VMEM),
        scratch_shapes=[
            pltpu.VMEM((5, TOK, HEADS * HEAD_DIM), bf),
            pltpu.VMEM((gate_table.shape[0], 256), f32),
            pltpu.VMEM((RING + 2, 256, 512), bf),
            pltpu.VMEM((2, 256, 256), bf),
            pltpu.VMEM((2, 384, HEAD_DIM), f32),
            pltpu.VMEM((2, 384, HEAD_DIM), f32),
            pltpu.VMEM((2, 384, HEAD_DIM), f32),
            pltpu.VMEM((384, HEAD_DIM), f32),
            pltpu.VMEM((384, HEAD_DIM), f32),
            pltpu.VMEM((384, HEAD_DIM), f32),
            pltpu.VMEM((384, HEAD_DIM), bf),
            pltpu.VMEM((TOK, HEADS * HEAD_DIM), bf),
            dma((5,)), dma, dma, dma, dma, dma, dma((2,)), dma((2,)),
            dma, dma, dma((2,)), dma, dma((RING,)), dma((2,)), dma((2,)), dma, dma,
        ],
        compiler_params=pltpu.CompilerParams(collective_id=0, has_side_effects=True),
    )(queries, keys_new, values_new, keys_old, values_old, gate_table, step_index)


def solution(mesh):
    tokens = P(("patch", "uly"), None)
    return jax.shard_map(
        body, mesh=mesh, in_specs=(tokens,) * 5 + (P(), P()), out_specs=tokens, check_vma=False
    )
```

time: 315 us -> 77.5 us (0.25)
  waiting for transfers between devices: 217 us -> 0 us
  Pallas kernels: 0 us -> 75.1 us
  starting transfers between devices: 30.4 us -> 0 us
  matrix products: 18.3 us -> 0 us
  local copies, waits for them, and re-layouts: 19.1 us -> 1.54 us
  between operations: 14.1 us -> 0.66 us
  blocking collectives: 12.5 us -> 0 us
    all_gather x1 -> x0, waiting for transfers between devices: 168 us -> none  [sent_together(): result, at, outs = (lax.all_gather(both, axis, axis=dim, tiled=True), 0, [])]
    pallas_call x0 -> x1, Pallas kernels: none -> 75.1 us  [body(): pl.pallas_call(kernel, out_shape=jax.ShapeDtypeStruct(queries.shape, bf),...]
    all_to_all x5 -> x0, waiting for transfers between devices: 49.2 us -> none  [the longest x1 12.8 us: body(): lax.all_to_all(keys_new, 'uly', split_axis=1, concat_axis=0, tiled=True)]
    all_to_all x5 -> x0, starting transfers between devices: 30.4 us -> none  [the longest x1 13.1 us: body(): lax.all_to_all(keys_old, 'uly', split_axis=1, concat_axis=0, tiled=True)]
    dot_general x11 -> x0, matrix products: 18.3 us -> none  [the longest x4 9.42 us: absorb(): jnp.einsum('hpk,khd->phd', expo.astype(jnp.bfloat16), value_piece, prefer...]
    all_to_all x1 -> x0, blocking collectives: 12.5 us -> none  [body(): return lax.all_to_all(gated, 'uly', split_axis=0, concat_axis=1, tiled=True)]
    slice x1 -> x0, local copies, waits for them, and re-layouts: 10.1 us -> none  [sent_together(): outs.append(lax.slice_in_dim(result, at, at + a.shape[along], axis=along))]
    all_to_all x6 -> x0, local copies, waits for them, and re-layouts: 7.53 us -> none  [the longest x1 1.61 us: body(): lax.all_to_all(keys_old, 'uly', split_axis=1, concat_axis=0, tiled=True)]
  transfers between devices with their start and end apart: 6 -> 0, of which waited for: 6 -> 0; matrix products, arithmetic and copies ran while one was open for 2% -> 0% of each run, Pallas kernels for 0% -> 0%
where the time goes in v1:
time: 77.5 us; the launch traced here: 77.3 us
  Pallas kernels  75.1 us (97%)
  local copies, waits for them, and re-layouts  1.54 us (2%)
    pallas_call x1, Pallas kernels, body(): pl.pallas_call(kernel, out_shape=jax.ShapeDtypeStruct(queries.shape, bf),...  75.1 us

profile of v1, /device:TPU:1, one launch (start us, length us, event | category | flops | bytes accessed | tf_op | source)
XLA Modules:
  0.0 77.3 jit_solution(6214828535727372687)
XLA Ops:
  0.7 75.1 %shard_map.73 = bf16[16,3072]{1,0:T(8,128)(2,1)} custom-call(bf16[16,3072]{1,0:T(8,128)(2,1)} %q_in.1, bf16[16,3072]{1,0:T(8,128)(2,1)} %kn_in.1, bf16[16,3072]{1,0:T(8,128)(2,1)} %vn_in.1, bf16[16,3072]{1,0:T(8,128)(2,1)} %ko_in.1, bf16[16,3072]{1,0:T(8,128)(2,1)} %vo_in.1, f32[50,3072]{1,0:T(8,128)} %gate_in.1, s32[1]{0:T(128)S(6)} %copy.9.step_ref), custom_call_target="tpu_custom_call" | custom-call | tf_op jit(solution)/shard_map/pallas_call | solution.py:356
  75.8 1.5 %copy.10 = bf16[16,3072]{1,0:T(8,128)(2,1)} copy(bf16[16,3072]{1,0:T(8,128)(2,1)} %shard_map.73) | data formatting | bytes 196608

commit v2 on v1

v2 whole, which is shorter than its diff:
```python
import jax
import jax.numpy as jnp
from jax import lax
from jax.experimental import pallas as pl
from jax.experimental.pallas import tpu as pltpu
from jax.sharding import PartitionSpec as P

HEADS = 24
HEAD_DIM = 128
MESH = pl.DeviceIdType.MESH
TOK = 16
RING = 16
SIDE = 4
C = HEAD_DIM ** (-0.5) * 1.4426950408889634

ORDER = (
    (0, 0), (1, 0), (3, 0), (0, 1), (0, 3), (2, 0), (1, 1), (1, 3),
    (3, 1), (3, 3), (0, 2), (2, 1), (2, 3), (1, 2), (3, 2), (2, 2),
)
SLOT = {pair: at for at, pair in enumerate(ORDER)}
HALF = (slice(0, 128), slice(128, 256))
MAIN, SHARED = 0, 1
OTHER, OWN = 0, 1
AHEAD, EVEN = 3, 6
OWN_STEP = 11


def kernel(
    q_in, kn_in, vn_in, ko_in, vo_in, gate_in, step_ref, out_ref,
    raw, pairs, gbuf, kv, qa, acc_m, acc_s, st_m, st_s, racc_m, racc_s, rst_m, rst_s, obuf, outbuf,
    stage_sem, gate_sem, kv_send, kv_recv, q_send, q_recv, qf_send, qf_recv,
    new_send, new_recv, old_sem, xy_send, xy_recv, part_send, part_recv, out_send, out_recv,
):
    p = lax.axis_index("patch")
    zl = lax.axis_index("uly")
    c = lax.rem(p, 2)
    y = lax.rem(p // 2, SIDE)
    zh = lax.rem(p // 8, 2)
    x = p // 16
    z = zh * 8 + zl
    g, s = z // 2, lax.rem(z, 2)

    def patch_of(x_, zh_, y_, c_):
        return ((x_ * 2 + zh_) * SIDE + y_) * 2 + c_

    def z_dev(z_):
        return {"patch": patch_of(x, z_ // 8, y, c), "uly": lax.rem(z_, 8)}

    def xy_dev(da, db):
        x_ = lax.rem(x + da * (1 - c) + db * c, SIDE)
        y_ = lax.rem(y + da * c + db * (1 - c), SIDE)
        return {"patch": patch_of(x_, zh, y_, c), "uly": zl}

    partner = {"patch": patch_of(x, zh, y, 1 - c), "uly": zl}

    def lanes(at, n=HEAD_DIM):
        return pl.ds(pl.multiple_of(at, HEAD_DIM), n)

    def rows(at, n):
        return pl.ds(pl.multiple_of(at, TOK), n)

    def remote(src, dst, ssem, rsem, dev):
        return pltpu.make_async_remote_copy(
            src_ref=src, dst_ref=dst, send_sem=ssem, recv_sem=rsem, device_id=dev, device_id_type=MESH
        )

    loads = [
        pltpu.make_async_copy(ref, raw.at[at], stage_sem.at[at])
        for at, ref in enumerate((ko_in, vo_in, kn_in, vn_in, q_in))
    ]
    for load in loads:
        load.start()
    gate_load = pltpu.make_async_copy(gate_in.at[:, lanes((3 * g + s) * HEAD_DIM, 256)], gbuf, gate_sem)
    gate_load.start()

    barrier = pltpu.get_barrier_semaphore()

    def greet(d, carry):
        pl.semaphore_signal(barrier, inc=1, device_id=z_dev(lax.rem(z + d, RING)), device_id_type=MESH)
        return carry

    lax.fori_loop(1, RING, greet, 0)
    for da, db in ((1, 0), (3, 0), (0, 1), (0, 3)):
        pl.semaphore_signal(barrier, inc=1, device_id=xy_dev(da, db), device_id_type=MESH)
    pl.semaphore_signal(barrier, inc=1, device_id=partner, device_id_type=MESH)
    for ref in (acc_m, acc_s):
        ref[...] = jnp.zeros_like(ref)
    for ref in (st_m, st_s):
        at = lax.broadcasted_iota(jnp.int32, ref.shape, 1)
        ref[...] = jnp.where(at == 0, -1e30, 0.0)
    for load in loads:
        load.wait()
    for at in range(4):
        for head in range(HEADS):
            col = (2 * head + at % 2) * HEAD_DIM
            pairs[at // 2, :, col:col + HEAD_DIM] = raw[at, :, head * HEAD_DIM:(head + 1) * HEAD_DIM]
    pl.semaphore_wait(barrier, RING - 1 + 4 + 1)

    mine = rows(z * TOK, TOK)

    def far(i):
        return lax.rem(z + 8 + ((i + 1) // 2) * (2 * lax.rem(i, 2) - 1), RING)

    def head_of(z_, which):
        group = 3 * (z_ // 2)
        return group + 1 if which == SHARED else group + 2 * lax.rem(z_, 2)

    def pair_of(z_, which):
        return lanes(256 * head_of(z_, which), 256)

    def single_of(z_, which):
        return lanes(HEAD_DIM * head_of(z_, which))

    def to_all(one):
        def step(i, carry):
            one(far(i))
            return carry

        lax.fori_loop(0, RING - 1, step, 0)

    def send_old(which):
        to_all(lambda t: remote(
            pairs.at[0, :, pair_of(t, which)], kv.at[which, 0, mine, :],
            kv_send.at[which], kv_recv.at[which], z_dev(t),
        ).start())
        pltpu.make_async_copy(
            pairs.at[0, :, pair_of(z, which)], kv.at[which, 0, mine, :], kv_recv.at[which]
        ).start()

    q_cols = (slice(0, 128), slice(128, 256))

    def send_q(t):
        remote(
            raw.at[4, :, single_of(t, MAIN)], qa.at[OWN, mine, q_cols[MAIN]], q_send, q_recv, z_dev(t)
        ).start()

        @pl.when(lax.rem(t, 2) == zh)
        def _():
            remote(
                raw.at[4, :, single_of(t, SHARED)], qa.at[OWN, mine, q_cols[SHARED]], q_send, q_recv, z_dev(t)
            ).start()

    def send_new(t):
        remote(
            pairs.at[1, :, pair_of(t, MAIN)], kv.at[MAIN, RING + zh, mine, :],
            new_send, new_recv.at[MAIN], z_dev(t),
        ).start()

    def send_new_shared(t):
        @pl.when(lax.rem(t, 2) == zh)
        def _():
            remote(
                pairs.at[1, :, pair_of(t, SHARED)], kv.at[SHARED, RING + zh, mine, :],
                new_send, new_recv.at[SHARED], z_dev(t),
            ).start()

    send_old(MAIN)
    send_old(SHARED)

    def start_queries():
        to_all(send_q)
        pltpu.make_async_copy(raw.at[4, :, single_of(z, MAIN)], qa.at[OWN, mine, q_cols[MAIN]], q_recv).start()

        @pl.when(s == zh)
        def _():
            pltpu.make_async_copy(
                raw.at[4, :, single_of(z, SHARED)], qa.at[OWN, mine, q_cols[SHARED]], q_recv
            ).start()

    def start_new():
        to_all(send_new)
        pltpu.make_async_copy(
            pairs.at[1, :, pair_of(z, MAIN)], kv.at[MAIN, RING + zh, mine, :], new_recv.at[MAIN]
        ).start()
        to_all(send_new_shared)

        @pl.when(s == zh)
        def _():
            pltpu.make_async_copy(
                pairs.at[1, :, pair_of(z, SHARED)], kv.at[SHARED, RING + zh, mine, :], new_recv.at[SHARED]
            ).start()


    def push(which, src, dst, da, db, part=None):
        a, b = kv.at[which, SLOT[src]], kv.at[which, SLOT[dst]]
        if part is not None:
            a, b = kv.at[which, SLOT[src], HALF[part]], kv.at[which, SLOT[dst], HALF[part]]
        remote(a, b, xy_send, xy_recv.at[which, SLOT[dst]], xy_dev(da, db)).start()

    def pass_on(which, pair):
        da, db = pair
        if pair == (0, 0):
            push(which, pair, (1, 0), 1, 0)
            push(which, pair, (3, 0), 3, 0)
        if pair == (1, 0):
            push(which, pair, (2, 0), 1, 0, 0)
        if pair == (3, 0):
            push(which, pair, (2, 0), 3, 0, 1)
        if db == 0:
            push(which, pair, (da, 1), 0, 1)
            push(which, pair, (da, 3), 0, 3)
        if db == 1:
            push(which, pair, (da, 2), 0, 1, 0)
        if db == 3:
            push(which, pair, (da, 2), 0, 3, 1)

    def begin(which):
        whole = kv.at[which, 0]
        pltpu.make_async_copy(whole, whole, kv_recv.at[which]).wait()
        pass_on(which, (0, 0))
        for side in range(2):
            keep = HALF[1 - side]
            pltpu.make_async_copy(
                kv.at[which, 0, keep], kv.at[which, RING + side, keep], old_sem.at[which, side]
            ).start()

    def arrived(which, k):
        pltpu.make_async_copy(kv.at[which, k], kv.at[which, k], xy_recv.at[which, k]).wait()

    def take(k, first, last):
        for which in range(2):
            arrived(which, k)
            for at in range(first, last):
                if ORDER[at][1] != 2:
                    @pl.when(k == at)
                    def _(pair=ORDER[at]):
                        pass_on(which, pair)

    begin(MAIN)
    begin(SHARED)
    start_queries()
    start_new()
    for k in range(1, AHEAD + 1):
        for which in range(2):
            arrived(which, k)
            pass_on(which, ORDER[k])

    pltpu.make_async_copy(qa.at[OWN, 0:192], qa.at[OWN, 0:192], q_recv).wait()
    shared_rows = rows(s * 128, 128)
    q_main = remote(
        qa.at[OWN, :, q_cols[MAIN]], qa.at[OTHER, :, q_cols[MAIN]], qf_send.at[0], qf_recv.at[0], partner
    )
    q_shared = remote(
        qa.at[OWN, shared_rows, q_cols[SHARED]], qa.at[OTHER, shared_rows, q_cols[SHARED]],
        qf_send.at[1], qf_recv.at[1], partner,
    )
    q_main.start()
    q_shared.start()
    q_main.wait()
    q_shared.wait()

    def absorb(acc, st, core, across, queries, block):
        keys, values = block[:, :HEAD_DIM], block[:, HEAD_DIM:]
        dots = lax.dot_general(keys, queries, (((1,), (1,)), ((), ())), preferred_element_type=jnp.float32)
        old = st[core, 0:1, across]
        new = jnp.maximum(old, jnp.max(dots, axis=0, keepdims=True))
        shrink = jnp.exp2((old - new) * C)
        expo = jnp.exp2((dots - new) * C)
        st[core, 1:2, across] = st[core, 1:2, across] * shrink + jnp.sum(expo, axis=0, keepdims=True)
        acc[core, :, across] = acc[core, :, across] * shrink + lax.dot_general(
            values, expo.astype(jnp.bfloat16), (((0,), (0,)), ((), ())), preferred_element_type=jnp.float32
        )
        st[core, 0:1, across] = new

    def main_chunk(core, k):
        absorb(acc_m, st_m, core, slice(0, 256), qa[core, :, q_cols[MAIN]], kv.at[MAIN, k])

    def shared_chunk(core, k):
        absorb(acc_s, st_s, core, slice(0, 128), qa[core, shared_rows, q_cols[SHARED]], kv.at[SHARED, k])

    def whole(k):
        jobs = [
            (acc, st, core, queries, kv.at[which, k])
            for core in (OTHER, OWN)
            for acc, st, which, queries in (
                (acc_m, st_m, MAIN, qa[core, :, q_cols[MAIN]]),
                (acc_s, st_s, SHARED, qa[core, shared_rows, q_cols[SHARED]]),
            )
        ]
        scored, mixed = [], []
        for acc, st, core, queries, block in jobs:
            dots = lax.dot_general(
                block[:, :HEAD_DIM], queries, (((1,), (1,)), ((), ())), preferred_element_type=jnp.float32
            )
            scored.append((dots, jnp.maximum(st[core, 0:1], jnp.max(dots, axis=0, keepdims=True))))
        for (acc, st, core, queries, block), (dots, new) in zip(jobs, scored):
            expo = jnp.exp2((dots - new) * C)
            shrink = jnp.exp2((st[core, 0:1] - new) * C)
            mixed.append((shrink, jnp.sum(expo, axis=0, keepdims=True), lax.dot_general(
                block[:, HEAD_DIM:], expo.astype(jnp.bfloat16), (((0,), (0,)), ((), ())),
                preferred_element_type=jnp.float32,
            )))
        for (acc, st, core, queries, block), (dots, new), (shrink, added, update) in zip(jobs, scored, mixed):
            st[core, 1:2] = st[core, 1:2] * shrink + added
            acc[core] = acc[core] * shrink + update
            st[core, 0:1] = new

    def own_ready(which, count):
        got = kv.at[which, RING, 0:count]
        pltpu.make_async_copy(got, got, new_recv.at[which]).wait()
        for side in range(2):
            keep = HALF[1 - side]
            pltpu.make_async_copy(
                kv.at[which, 0, keep], kv.at[which, RING + side, keep], old_sem.at[which, side]
            ).wait()

    def partial(which):
        acc, st, racc, rst = ((acc_m, st_m, racc_m, rst_m), (acc_s, st_s, racc_s, rst_s))[which]
        return [
            remote(acc.at[OTHER], racc, part_send.at[which, 0], part_recv.at[which, 0], partner),
            remote(st.at[OTHER], rst, part_send.at[which, 1], part_recv.at[which, 1], partner),
        ]

    gate_load.wait()
    picked = lax.broadcasted_iota(jnp.int32, gbuf.shape, 0) == step_ref[0]
    gate = jnp.sum(jnp.where(picked, gbuf[...], 0.0), axis=0, keepdims=True)
    gate_lo, gate_hi = gate[:, :HEAD_DIM], gate[:, HEAD_DIM:]
    gates = (jnp.where(s == 0, gate_lo, gate_hi), jnp.where(s == 0, gate_hi, gate_lo))

    def merge(which):
        acc, st, racc, rst = ((acc_m, st_m, racc_m, rst_m), (acc_s, st_s, racc_s, rst_s))[which]
        for copy in partial(which):
            copy.wait()
        m1, l1, m2, l2 = st[OWN, 0:1], st[OWN, 1:2], rst[0:1], rst[1:2]
        top = jnp.maximum(m1, m2)
        w1, w2 = jnp.exp2((m1 - top) * C), jnp.exp2((m2 - top) * C)
        total = l1 * w1 + l2 * w2
        mixed = acc[OWN] * (w1 / total) + racc[...] * (w2 / total)
        first = 256 * which
        obuf[first:first + mixed.shape[1]] = (jnp.transpose(mixed) * gates[which]).astype(jnp.bfloat16)

    my_main, my_shared = single_of(z, MAIN), single_of(z, SHARED)

    def out_main():
        merge(MAIN)
        to_all(lambda t: remote(
            obuf.at[rows(t * TOK, TOK)], outbuf.at[:, my_main], out_send, out_recv, z_dev(t)
        ).start())
        pltpu.make_async_copy(obuf.at[mine], outbuf.at[:, my_main], out_recv).start()

    def out_shared():
        merge(SHARED)

        def one(t):
            @pl.when(t // 8 == s)
            def _():
                remote(
                    obuf.at[rows(256 + lax.rem(t, 8) * TOK, TOK)], outbuf.at[:, my_shared],
                    out_send, out_recv, z_dev(t),
                ).start()

        to_all(one)

        @pl.when(zh == s)
        def _():
            pltpu.make_async_copy(
                obuf.at[rows(256 + zl * TOK, TOK)], outbuf.at[:, my_shared], out_recv
            ).start()

    def both(core, k):
        main_chunk(core, k)
        shared_chunk(core, k)

    def catch_up(i, carry):
        take(AHEAD + 1 + i, AHEAD + 1, EVEN + 1)

        def one(j, inner):
            whole(1 + 2 * i + j)
            return inner

        lax.fori_loop(0, 2, one, 0)
        return carry

    def keep_up(k, carry):
        take(k, EVEN + 1, RING)

        @pl.when(k == OWN_STEP)
        def _():
            own_ready(MAIN, 256)
            own_ready(SHARED, 128)
            both(OTHER, 0)
            for side in range(2):
                absorb(
                    acc_m, st_m, OWN, HALF[side], qa[OWN, HALF[side], q_cols[MAIN]], kv.at[MAIN, RING + side]
                )
            shared_chunk(OWN, RING + s)

        whole(k)
        return carry

    lax.fori_loop(0, EVEN - AHEAD, catch_up, 0)
    lax.fori_loop(EVEN + 1, RING, keep_up, 0)
    for which in range(2):
        for copy in partial(which):
            copy.start()
    out_main()
    out_shared()

    def sent(ref, sem):
        pltpu.make_async_copy(ref, ref, sem).wait()

    for which in range(2):
        sent(kv.at[which, 0, 0:240], kv_send.at[which])
        sent(kv.at[which, pl.ds(1, 15)], xy_send)

    @pl.when(zh == s)
    def _():
        sent(qa.at[0, 0:176], q_send)
        sent(obuf.at[pl.ds(0, 22 * TOK)], out_send)
        sent(kv.at[MAIN, 0], new_send)
        sent(kv.at[MAIN, 0, 0:96], new_send)

    @pl.when(zh != s)
    def _():
        sent(qa.at[0, 0:184], q_send)
        sent(obuf.at[pl.ds(0, 23 * TOK)], out_send)
        sent(kv.at[MAIN, 0], new_send)
        sent(kv.at[MAIN, 0, 0:112], new_send)

    pltpu.make_async_copy(outbuf, outbuf, out_recv).wait()
    out_ref[...] = outbuf[...]


def body(queries, keys_new, values_new, keys_old, values_old, gate_table, step_index):
    bf, f32 = jnp.bfloat16, jnp.float32
    dma = pltpu.SemaphoreType.DMA
    width = HEADS * HEAD_DIM
    return pl.pallas_call(
        kernel,
        out_shape=jax.ShapeDtypeStruct(queries.shape, bf),
        in_specs=[pl.BlockSpec(memory_space=pl.ANY)] * 6 + [pl.BlockSpec(memory_space=pltpu.SMEM)],
        out_specs=pl.BlockSpec(memory_space=pltpu.VMEM),
        scratch_shapes=[
            pltpu.VMEM((5, TOK, width), bf),
            pltpu.VMEM((2, TOK, 2 * width), bf),
            pltpu.VMEM((gate_table.shape[0], 256), f32),
            pltpu.VMEM((2, RING + 2, 256, 256), bf),
            pltpu.VMEM((2, 256, 256), bf),
            pltpu.VMEM((2, HEAD_DIM, 256), f32),
            pltpu.VMEM((2, HEAD_DIM, 128), f32),
            pltpu.VMEM((2, 8, 256), f32),
            pltpu.VMEM((2, 8, 128), f32),
            pltpu.VMEM((HEAD_DIM, 256), f32),
            pltpu.VMEM((HEAD_DIM, 128), f32),
            pltpu.VMEM((8, 256), f32),
            pltpu.VMEM((8, 128), f32),
            pltpu.VMEM((384, HEAD_DIM), bf),
            pltpu.VMEM((TOK, width), bf),
            dma((5,)), dma, dma((2,)), dma((2,)), dma, dma, dma((2,)), dma((2,)),
            dma, dma((2,)), dma((2, 2)), dma, dma((2, RING)), dma((2, 2)), dma((2, 2)), dma, dma,
        ],
        compiler_params=pltpu.CompilerParams(collective_id=0, has_side_effects=True),
    )(queries, keys_new, values_new, keys_old, values_old, gate_table, step_index)


def solution(mesh):
    tokens = P(("patch", "uly"), None)
    return jax.shard_map(
        body, mesh=mesh, in_specs=(tokens,) * 5 + (P(), P()), out_specs=tokens, check_vma=False
    )
```

time: 77.5 us -> 69.2 us (0.89)
  Pallas kernels: 75.1 us -> 66.5 us
    pallas_call x1, Pallas kernels: 75.1 us -> 66.5 us  [body(): pl.pallas_call(kernel, out_shape=jax.ShapeDtypeStruct(queries.shape, bf),...]
where the time goes in v2:
time: 69.2 us; the launch traced here: 68.7 us
  Pallas kernels  66.5 us (96%)
  local copies, waits for them, and re-layouts  1.54 us (2%)
    pallas_call x1, Pallas kernels, body(): pl.pallas_call(kernel, out_shape=jax.ShapeDtypeStruct(queries.shape, bf),...  66.5 us
    unnamed x1, local copies, waits for them, and re-layouts  1.54 us

profile of v2, /device:TPU:1, one launch (start us, length us, event | category | flops | bytes accessed | tf_op | source)
XLA Modules:
  0.0 68.7 jit_solution(9962941035489716968)
XLA Ops:
  0.7 66.5 %shard_map.73 = bf16[16,3072]{1,0:T(8,128)(2,1)} custom-call(bf16[16,3072]{1,0:T(8,128)(2,1)} %q_in.1, bf16[16,3072]{1,0:T(8,128)(2,1)} %kn_in.1, bf16[16,3072]{1,0:T(8,128)(2,1)} %vn_in.1, bf16[16,3072]{1,0:T(8,128)(2,1)} %ko_in.1, bf16[16,3072]{1,0:T(8,128)(2,1)} %vo_in.1, f32[50,3072]{1,0:T(8,128)} %gate_in.1, s32[1]{0:T(128)S(6)} %copy.9.step_ref), custom_call_target="tpu_custom_call" | custom-call | tf_op jit(solution)/shard_map/pallas_call | solution.py:428
  67.2 1.5 %copy.10 = bf16[16,3072]{1,0:T(8,128)(2,1)} copy(bf16[16,3072]{1,0:T(8,128)(2,1)} %shard_map.73) | data formatting | bytes 196608

commit v3 on v2

v3 whole, which is shorter than its diff:
```python
import jax
import jax.numpy as jnp
from jax import lax
from jax.experimental import pallas as pl
from jax.experimental.pallas import tpu as pltpu
from jax.sharding import PartitionSpec as P

HEADS = 24
HEAD_DIM = 128
MESH = pl.DeviceIdType.MESH
TOK = 16
RING = 16
SIDE = 4
C = HEAD_DIM ** (-0.5) * 1.4426950408889634

ORDER = (
    (0, 0), (1, 0), (3, 0), (0, 1), (0, 3), (2, 0), (1, 1), (1, 3),
    (3, 1), (3, 3), (0, 2), (2, 1), (2, 3), (1, 2), (3, 2), (2, 2),
)
SLOT = {pair: at for at, pair in enumerate(ORDER)}
HALF = (slice(0, 128), slice(128, 256))
QUARTER = (slice(0, 64), slice(64, 128))
MAIN, SHARED = 0, 1
OTHER, OWN = 0, 1
AHEAD, EVEN, LEAD = 3, 6, 3


def kernel(
    q_in, kn_in, vn_in, ko_in, vo_in, gate_in, step_ref, out_ref,
    raw, pairs, gbuf, km, ks, qm, qs, acc_m, acc_s, st_m, st_s, racc_m, racc_s, rst_m, rst_s, obuf, outbuf,
    stage_sem, gate_sem, kv_send, kv_recv, q_send, q_recv, qf_send, qf_recv,
    new_send, new_recv, old_sem, xy_send, xy_recv, part_send, part_recv, out_send, out_recv,
):
    p = lax.axis_index("patch")
    zl = lax.axis_index("uly")
    c = lax.rem(p, 2)
    y = lax.rem(p // 2, SIDE)
    zh = lax.rem(p // 8, 2)
    x = p // 16
    z = zh * 8 + zl
    g, s = z // 2, lax.rem(z, 2)

    def patch_of(x_, zh_, y_, c_):
        return ((x_ * 2 + zh_) * SIDE + y_) * 2 + c_

    def z_dev(z_):
        return {"patch": patch_of(x, z_ // 8, y, c), "uly": lax.rem(z_, 8)}

    def xy_dev(da, db):
        x_ = lax.rem(x + da * (1 - c) + db * c, SIDE)
        y_ = lax.rem(y + da * c + db * (1 - c), SIDE)
        return {"patch": patch_of(x_, zh, y_, c), "uly": zl}

    partner = {"patch": patch_of(x, zh, y, 1 - c), "uly": zl}
    beside = {"patch": patch_of(x, zh, y, c), "uly": zl + 1 - 2 * s}
    across = {"patch": patch_of(x, zh, y, 1 - c), "uly": zl + 1 - 2 * s}
    kv, qa = (km, ks), (qm, qs)

    def lanes(at, n=HEAD_DIM):
        return pl.ds(pl.multiple_of(at, HEAD_DIM), n)

    def rows(at, n):
        return pl.ds(pl.multiple_of(at, TOK), n)

    def remote(src, dst, ssem, rsem, dev):
        return pltpu.make_async_remote_copy(
            src_ref=src, dst_ref=dst, send_sem=ssem, recv_sem=rsem, device_id=dev, device_id_type=MESH
        )

    loads = [
        pltpu.make_async_copy(ref, raw.at[at], stage_sem.at[at])
        for at, ref in enumerate((ko_in, vo_in, kn_in, vn_in, q_in))
    ]
    for load in loads:
        load.start()
    gate_load = pltpu.make_async_copy(gate_in.at[:, lanes((3 * g + s) * HEAD_DIM, 256)], gbuf, gate_sem)
    gate_load.start()

    barrier = pltpu.get_barrier_semaphore()

    def greet(d, carry):
        pl.semaphore_signal(barrier, inc=1, device_id=z_dev(lax.rem(z + d, RING)), device_id_type=MESH)
        return carry

    lax.fori_loop(1, RING, greet, 0)
    for da, db in ((1, 0), (3, 0), (0, 1), (0, 3)):
        pl.semaphore_signal(barrier, inc=1, device_id=xy_dev(da, db), device_id_type=MESH)
    for dev in (partner, across):
        pl.semaphore_signal(barrier, inc=1, device_id=dev, device_id_type=MESH)
    for ref in (acc_m, acc_s):
        ref[...] = jnp.zeros_like(ref)
    for ref in (st_m, st_s):
        at = lax.broadcasted_iota(jnp.int32, ref.shape, 1)
        ref[...] = jnp.where(at == 0, -1e30, 0.0)
    for load in loads:
        load.wait()
    for at in range(4):
        for head in range(HEADS):
            col = (2 * head + at % 2) * HEAD_DIM
            pairs[at // 2, :, col:col + HEAD_DIM] = raw[at, :, head * HEAD_DIM:(head + 1) * HEAD_DIM]
    pl.semaphore_wait(barrier, RING - 1 + 4 + 2)

    mine, here = rows(z * TOK, TOK), rows(zl * TOK, TOK)

    def far(i):
        return lax.rem(z + 8 + ((i + 1) // 2) * (2 * lax.rem(i, 2) - 1), RING)

    def head_of(z_, which):
        group = 3 * (z_ // 2)
        return group + 1 if which == SHARED else group + 2 * lax.rem(z_, 2)

    def pair_of(z_, which):
        return lanes(256 * head_of(z_, which), 256)

    def single_of(z_, which):
        return lanes(HEAD_DIM * head_of(z_, which))

    def to_all(one):
        def step(i, carry):
            one(far(i))
            return carry

        lax.fori_loop(0, RING - 1, step, 0)

    def query_rows(z_):
        return rows(lax.rem(zh + z_, 2) * 128 + zl * TOK, TOK)

    def send_old_main(t):
        remote(
            pairs.at[0, :, pair_of(t, MAIN)], km.at[0, mine, :], kv_send.at[MAIN], kv_recv.at[MAIN], z_dev(t)
        ).start()

    def send_old_shared(t):
        @pl.when(lax.rem(t, 2) == zh)
        def _():
            remote(
                pairs.at[0, :, pair_of(t, SHARED)], ks.at[0, here, :],
                kv_send.at[SHARED], kv_recv.at[SHARED], z_dev(t),
            ).start()

    def send_q(t):
        remote(raw.at[4, :, single_of(t, MAIN)], qm.at[OWN, mine, :], q_send.at[MAIN], q_recv.at[MAIN], z_dev(t)).start()
        remote(
            raw.at[4, :, single_of(t, SHARED)], qs.at[OWN, query_rows(t), :],
            q_send.at[SHARED], q_recv.at[SHARED], z_dev(t),
        ).start()

    def send_new(t):
        remote(
            pairs.at[1, :, pair_of(t, MAIN)], km.at[RING + zh, mine, :],
            new_send.at[MAIN], new_recv.at[MAIN], z_dev(t),
        ).start()

    def send_new_shared(t):
        @pl.when(lax.rem(t, 2) == zh)
        def _():
            remote(
                pairs.at[1, :, pair_of(t, SHARED)], ks.at[RING, here, :],
                new_send.at[SHARED], new_recv.at[SHARED], z_dev(t),
            ).start()

    to_all(send_old_shared)
    to_all(send_old_main)
    pltpu.make_async_copy(pairs.at[0, :, pair_of(z, MAIN)], km.at[0, mine, :], kv_recv.at[MAIN]).start()

    @pl.when(s == zh)
    def _():
        pltpu.make_async_copy(
            pairs.at[0, :, pair_of(z, SHARED)], ks.at[0, here, :], kv_recv.at[SHARED]
        ).start()

    def start_queries():
        to_all(send_q)
        pltpu.make_async_copy(raw.at[4, :, single_of(z, MAIN)], qm.at[OWN, mine, :], q_recv.at[MAIN]).start()
        pltpu.make_async_copy(
            raw.at[4, :, single_of(z, SHARED)], qs.at[OWN, query_rows(z), :], q_recv.at[SHARED]
        ).start()

    def start_new():
        to_all(send_new_shared)
        to_all(send_new)
        pltpu.make_async_copy(
            pairs.at[1, :, pair_of(z, MAIN)], km.at[RING + zh, mine, :], new_recv.at[MAIN]
        ).start()

        @pl.when(s == zh)
        def _():
            pltpu.make_async_copy(
                pairs.at[1, :, pair_of(z, SHARED)], ks.at[RING, here, :], new_recv.at[SHARED]
            ).start()

    def push(which, src, dst, da, db, part=None):
        a, b = kv[which].at[SLOT[src]], kv[which].at[SLOT[dst]]
        if part is not None:
            piece = (HALF, QUARTER)[which][part]
            a, b = kv[which].at[SLOT[src], piece], kv[which].at[SLOT[dst], piece]
        remote(a, b, xy_send.at[which], xy_recv.at[which, SLOT[dst]], xy_dev(da, db)).start()

    def pass_on(which, pair):
        da, db = pair
        if pair == (0, 0):
            push(which, pair, (1, 0), 1, 0)
            push(which, pair, (3, 0), 3, 0)
        if pair == (1, 0):
            push(which, pair, (2, 0), 1, 0, 0)
        if pair == (3, 0):
            push(which, pair, (2, 0), 3, 0, 1)
        if db == 0:
            push(which, pair, (da, 1), 0, 1)
            push(which, pair, (da, 3), 0, 3)
        if db == 1:
            push(which, pair, (da, 2), 0, 1, 0)
        if db == 3:
            push(which, pair, (da, 2), 0, 3, 1)

    def begin(which):
        whole = kv[which].at[0]
        pltpu.make_async_copy(whole, whole, kv_recv.at[which]).wait()
        pass_on(which, (0, 0))

    def arrived(which, k):
        pltpu.make_async_copy(kv[which].at[k], kv[which].at[k], xy_recv.at[which, k]).wait()

    def take(which, k, first, last):
        arrived(which, k)
        for at in range(first, last):
            if ORDER[at][1] != 2:
                @pl.when(k == at)
                def _(pair=ORDER[at]):
                    pass_on(which, pair)

    begin(SHARED)
    begin(MAIN)
    start_queries()
    start_new()
    for side in range(2):
        keep = HALF[1 - side]
        pltpu.make_async_copy(km.at[0, keep], km.at[RING + side, keep], old_sem.at[side]).start()
    for k in range(1, AHEAD + LEAD + 1):
        for which, at in ((SHARED, k), (MAIN, k - LEAD)):
            if at >= 1:
                arrived(which, at)
                if ORDER[at][1] != 2:
                    pass_on(which, ORDER[at])

    for which in range(2):
        pltpu.make_async_copy(qa[which].at[OWN], qa[which].at[OWN], q_recv.at[which]).wait()
    over = [
        remote(qa[which].at[OWN], qa[which].at[OTHER], qf_send.at[which], qf_recv.at[which], partner)
        for which in range(2)
    ]
    for copy in over:
        copy.start()
    for copy in over:
        copy.wait()

    def absorb(jobs):
        scored, mixed = [], []
        for acc, st, at, queries, block in jobs:
            dots = lax.dot_general(
                block[:, :HEAD_DIM], queries, (((1,), (1,)), ((), ())), preferred_element_type=jnp.float32
            )
            core, cols = at
            scored.append((dots, jnp.maximum(st[core, 0:1, cols], jnp.max(dots, axis=0, keepdims=True))))
        for (acc, st, (core, cols), queries, block), (dots, new) in zip(jobs, scored):
            expo = jnp.exp2((dots - new) * C)
            shrink = jnp.exp2((st[core, 0:1, cols] - new) * C)
            mixed.append((shrink, jnp.sum(expo, axis=0, keepdims=True), lax.dot_general(
                block[:, HEAD_DIM:], expo.astype(jnp.bfloat16), (((0,), (0,)), ((), ())),
                preferred_element_type=jnp.float32,
            )))
        for (acc, st, (core, cols), queries, block), (dots, new), (shrink, added, update) in zip(
            jobs, scored, mixed
        ):
            st[core, 1:2, cols] = st[core, 1:2, cols] * shrink + added
            acc[core, :, cols] = acc[core, :, cols] * shrink + update
            st[core, 0:1, cols] = new

    full = slice(0, 256)

    def main_jobs(k, cores=(OTHER, OWN)):
        return [(acc_m, st_m, (core, full), qm[core], km.at[k]) for core in cores]

    def shared_jobs(k, cores=(OTHER, OWN)):
        return [(acc_s, st_s, (core, full), qs[core], ks.at[k]) for core in cores]

    def own_main():
        got = km.at[RING, 0:256]
        pltpu.make_async_copy(got, got, new_recv.at[MAIN]).wait()
        for side in range(2):
            keep = HALF[1 - side]
            pltpu.make_async_copy(km.at[0, keep], km.at[RING + side, keep], old_sem.at[side]).wait()
        absorb(main_jobs(0, (OTHER,)) + [
            (acc_m, st_m, (OWN, HALF[side]), qm[OWN, HALF[side]], km.at[RING + side]) for side in range(2)
        ])

    def own_shared():
        pltpu.make_async_copy(ks.at[RING], ks.at[RING], new_recv.at[SHARED]).wait()
        absorb(shared_jobs(0, (OTHER,)) + [
            (acc_s, st_s, (OWN, HALF[0]), qs[OWN, HALF[0]], ks.at[RING]),
            (acc_s, st_s, (OWN, HALF[1]), qs[OWN, HALF[1]], ks.at[0]),
        ])

    main_parts = [
        remote(acc_m.at[OTHER], racc_m, part_send.at[0], part_recv.at[0], partner),
        remote(st_m.at[OTHER], rst_m, part_send.at[1], part_recv.at[1], partner),
    ]
    shared_parts = []
    for at, (core, cols, dev) in enumerate(
        ((OWN, HALF[1], beside), (OTHER, HALF[1], across), (OTHER, HALF[0], partner))
    ):
        shared_parts += [
            remote(
                acc_s.at[core, :, cols], racc_s.at[at], part_send.at[2 + at], part_recv.at[2 + at], dev
            ),
            remote(st_s.at[core, :, cols], rst_s.at[at], part_send.at[5 + at], part_recv.at[5 + at], dev),
        ]

    gate_load.wait()
    picked = lax.broadcasted_iota(jnp.int32, gbuf.shape, 0) == step_ref[0]
    gate = jnp.sum(jnp.where(picked, gbuf[...], 0.0), axis=0, keepdims=True)
    gate_lo, gate_hi = gate[:, :HEAD_DIM], gate[:, HEAD_DIM:]
    gates = (jnp.where(s == 0, gate_lo, gate_hi), jnp.where(s == 0, gate_hi, gate_lo))

    def merge(terms):
        top = terms[0][0]
        for m, _, _ in terms[1:]:
            top = jnp.maximum(top, m)
        scales = [jnp.exp2((m - top) * C) for m, _, _ in terms]
        total = sum(l * w for (_, l, _), w in zip(terms, scales))
        return sum(a * (w / total) for (_, _, a), w in zip(terms, scales))

    def finish(which, mixed):
        first = 256 * which
        obuf[first:first + mixed.shape[1]] = (jnp.transpose(mixed) * gates[which]).astype(jnp.bfloat16)

    my_main, my_shared = single_of(z, MAIN), single_of(z, SHARED)

    def out_main():
        for copy in main_parts:
            copy.wait()
        finish(MAIN, merge([
            (st_m[OWN, 0:1], st_m[OWN, 1:2], acc_m[OWN]), (rst_m[0:1], rst_m[1:2], racc_m[...]),
        ]))
        to_all(lambda t: remote(
            obuf.at[rows(t * TOK, TOK)], outbuf.at[:, my_main], out_send, out_recv, z_dev(t)
        ).start())
        pltpu.make_async_copy(obuf.at[mine], outbuf.at[:, my_main], out_recv).start()

    def out_shared():
        for copy in shared_parts:
            copy.wait()
        home = HALF[0]
        finish(SHARED, merge(
            [(st_s[OWN, 0:1, home], st_s[OWN, 1:2, home], acc_s[OWN, :, home])]
            + [(rst_s[at, 0:1], rst_s[at, 1:2], racc_s[at]) for at in range(3)]
        ))

        def one(t):
            @pl.when(t // 8 == s)
            def _():
                remote(
                    obuf.at[rows(256 + lax.rem(t, 8) * TOK, TOK)], outbuf.at[:, my_shared],
                    out_send, out_recv, z_dev(t),
                ).start()

        to_all(one)

        @pl.when(zh == s)
        def _():
            pltpu.make_async_copy(
                obuf.at[rows(256 + zl * TOK, TOK)], outbuf.at[:, my_shared], out_recv
            ).start()

    def lead(k, carry):
        absorb(shared_jobs(k))
        return carry

    def catch_up(i, carry):
        k = AHEAD + 1 + i
        take(SHARED, k + LEAD, AHEAD + LEAD + 1, EVEN + LEAD + 1)
        take(MAIN, k, AHEAD + 1, EVEN + 1)

        def one(j, inner):
            absorb(main_jobs(1 + 2 * i + j) + shared_jobs(1 + 2 * i + j + LEAD))
            return inner

        lax.fori_loop(0, 2, one, 0)
        return carry

    def keep_up(k, carry):
        take(SHARED, k + LEAD, EVEN + LEAD + 1, RING)
        take(MAIN, k, EVEN + 1, RING - LEAD)
        absorb(main_jobs(k) + shared_jobs(k + LEAD))
        return carry

    def trail(k, carry):
        take(MAIN, k, RING - LEAD, RING)
        absorb(main_jobs(k))
        return carry

    lax.fori_loop(1, LEAD + 1, lead, 0)
    lax.fori_loop(0, EVEN - AHEAD, catch_up, 0)
    lax.fori_loop(EVEN + 1, RING - LEAD, keep_up, 0)
    own_shared()
    for copy in shared_parts:
        copy.start()
    lax.fori_loop(RING - LEAD, RING, trail, 0)
    own_main()
    for copy in main_parts:
        copy.start()
    out_main()
    out_shared()

    def sent(ref, sem):
        pltpu.make_async_copy(ref, ref, sem).wait()

    sent(km.at[0, 0:240], kv_send.at[MAIN])
    for which in range(2):
        sent(kv[which].at[pl.ds(1, 15)], xy_send.at[which])
        sent(qa[which].at[OWN, 0:240], q_send.at[which])
    sent(km.at[0, 0:240], new_send.at[MAIN])

    @pl.when(zh == s)
    def _():
        sent(ks.at[0, 0:112], kv_send.at[SHARED])
        sent(ks.at[0, 0:112], new_send.at[SHARED])
        sent(obuf.at[pl.ds(0, 22 * TOK)], out_send)

    @pl.when(zh != s)
    def _():
        sent(ks.at[0], kv_send.at[SHARED])
        sent(ks.at[0], new_send.at[SHARED])
        sent(obuf.at[pl.ds(0, 23 * TOK)], out_send)

    pltpu.make_async_copy(outbuf, outbuf, out_recv).wait()
    out_ref[...] = outbuf[...]


def body(queries, keys_new, values_new, keys_old, values_old, gate_table, step_index):
    bf, f32 = jnp.bfloat16, jnp.float32
    dma = pltpu.SemaphoreType.DMA
    width = HEADS * HEAD_DIM
    return pl.pallas_call(
        kernel,
        out_shape=jax.ShapeDtypeStruct(queries.shape, bf),
        in_specs=[pl.BlockSpec(memory_space=pl.ANY)] * 6 + [pl.BlockSpec(memory_space=pltpu.SMEM)],
        out_specs=pl.BlockSpec(memory_space=pltpu.VMEM),
        scratch_shapes=[
            pltpu.VMEM((5, TOK, width), bf),
            pltpu.VMEM((2, TOK, 2 * width), bf),
            pltpu.VMEM((gate_table.shape[0], 256), f32),
            pltpu.VMEM((RING + 2, 256, 256), bf),
            pltpu.VMEM((RING + 1, 128, 256), bf),
            pltpu.VMEM((2, 256, HEAD_DIM), bf),
            pltpu.VMEM((2, 256, HEAD_DIM), bf),
            pltpu.VMEM((2, HEAD_DIM, 256), f32),
            pltpu.VMEM((2, HEAD_DIM, 256), f32),
            pltpu.VMEM((2, 8, 256), f32),
            pltpu.VMEM((2, 8, 256), f32),
            pltpu.VMEM((HEAD_DIM, 256), f32),
            pltpu.VMEM((3, HEAD_DIM, 128), f32),
            pltpu.VMEM((8, 256), f32),
            pltpu.VMEM((3, 8, 128), f32),
            pltpu.VMEM((384, HEAD_DIM), bf),
            pltpu.VMEM((TOK, width), bf),
            dma((5,)), dma, dma((2,)), dma((2,)), dma((2,)), dma((2,)), dma((2,)), dma((2,)),
            dma((2,)), dma((2,)), dma((2,)), dma((2,)), dma((2, RING)), dma((8,)), dma((8,)), dma, dma,
        ],
        compiler_params=pltpu.CompilerParams(collective_id=0, has_side_effects=True),
    )(queries, keys_new, values_new, keys_old, values_old, gate_table, step_index)


def solution(mesh):
    tokens = P(("patch", "uly"), None)
    return jax.shard_map(
        body, mesh=mesh, in_specs=(tokens,) * 5 + (P(), P()), out_specs=tokens, check_vma=False
    )
```

time: 69.2 us -> 65.4 us (0.945)
  Pallas kernels: 66.5 us -> 62.8 us
    pallas_call x1, Pallas kernels: 66.5 us -> 62.8 us  [body(): pl.pallas_call(kernel, out_shape=jax.ShapeDtypeStruct(queries.shape, bf),...]
where the time goes in v3:
time: 65.4 us; the launch traced here: 65 us
  Pallas kernels  62.8 us (96%)
  local copies, waits for them, and re-layouts  1.54 us (2%)
  between operations  0.66 us (1%)
    pallas_call x1, Pallas kernels, body(): pl.pallas_call(kernel, out_shape=jax.ShapeDtypeStruct(queries.shape, bf),...  62.8 us
    unnamed x1, local copies, waits for them, and re-layouts  1.54 us

profile of v3, /device:TPU:1, one launch (start us, length us, event | category | flops | bytes accessed | tf_op | source)
XLA Modules:
  0.0 65.0 jit_solution(17041956008041676599)
XLA Ops:
  0.7 62.8 %shard_map.73 = bf16[16,3072]{1,0:T(8,128)(2,1)} custom-call(bf16[16,3072]{1,0:T(8,128)(2,1)} %q_in.1, bf16[16,3072]{1,0:T(8,128)(2,1)} %kn_in.1, bf16[16,3072]{1,0:T(8,128)(2,1)} %vn_in.1, bf16[16,3072]{1,0:T(8,128)(2,1)} %ko_in.1, bf16[16,3072]{1,0:T(8,128)(2,1)} %vo_in.1, f32[50,3072]{1,0:T(8,128)} %gate_in.1, s32[1]{0:T(128)S(6)} %copy.9.step_ref), custom_call_target="tpu_custom_call" | custom-call | tf_op jit(solution)/shard_map/pallas_call | solution.py:444
  63.5 1.5 %copy.10 = bf16[16,3072]{1,0:T(8,128)(2,1)} copy(bf16[16,3072]{1,0:T(8,128)(2,1)} %shard_map.73) | data formatting | bytes 196608

commit v4 on v3

--- a/solution.py
+++ b/solution.py
@@ -256,20 +256,27 @@
 
     def absorb(jobs):
         scored, mixed = [], []
-        for acc, st, at, queries, block in jobs:
-            dots = lax.dot_general(
-                block[:, :HEAD_DIM], queries, (((1,), (1,)), ((), ())), preferred_element_type=jnp.float32
-            )
-            core, cols = at
-            scored.append((dots, jnp.maximum(st[core, 0:1, cols], jnp.max(dots, axis=0, keepdims=True))))
-        for (acc, st, (core, cols), queries, block), (dots, new) in zip(jobs, scored):
-            expo = jnp.exp2((dots - new) * C)
-            shrink = jnp.exp2((st[core, 0:1, cols] - new) * C)
-            mixed.append((shrink, jnp.sum(expo, axis=0, keepdims=True), lax.dot_general(
-                block[:, HEAD_DIM:], expo.astype(jnp.bfloat16), (((0,), (0,)), ((), ())),
-                preferred_element_type=jnp.float32,
-            )))
-        for (acc, st, (core, cols), queries, block), (dots, new), (shrink, added, update) in zip(
+        for acc, st, (core, cols), queries, blocks in jobs:
+            new, parts = st[core, 0:1, cols], []
+            for block in blocks:
+                dots = lax.dot_general(
+                    block[:, :HEAD_DIM], queries, (((1,), (1,)), ((), ())),
+                    preferred_element_type=jnp.float32,
+                )
+                new = jnp.maximum(new, jnp.max(dots, axis=0, keepdims=True))
+                parts.append(dots)
+            scored.append((parts, new))
+        for (acc, st, (core, cols), queries, blocks), (parts, new) in zip(jobs, scored):
+            shrink, added, update = jnp.exp2((st[core, 0:1, cols] - new) * C), 0.0, 0.0
+            for block, dots in zip(blocks, parts):
+                expo = jnp.exp2((dots - new) * C)
+                added = added + jnp.sum(expo, axis=0, keepdims=True)
+                update = update + lax.dot_general(
+                    block[:, HEAD_DIM:], expo.astype(jnp.bfloat16), (((0,), (0,)), ((), ())),
+                    preferred_element_type=jnp.float32,
+                )
+            mixed.append((shrink, added, update))
+        for (acc, st, (core, cols), queries, blocks), (parts, new), (shrink, added, update) in zip(
             jobs, scored, mixed
         ):
             st[core, 1:2, cols] = st[core, 1:2, cols] * shrink + added
@@ -278,11 +285,11 @@
 
     full = slice(0, 256)
 
-    def main_jobs(k, cores=(OTHER, OWN)):
-        return [(acc_m, st_m, (core, full), qm[core], km.at[k]) for core in cores]
-
-    def shared_jobs(k, cores=(OTHER, OWN)):
-        return [(acc_s, st_s, (core, full), qs[core], ks.at[k]) for core in cores]
+    def main_jobs(*slots, cores=(OTHER, OWN)):
+        return [(acc_m, st_m, (core, full), qm[core], [km.at[k] for k in slots]) for core in cores]
+
+    def shared_jobs(*slots, cores=(OTHER, OWN)):
+        return [(acc_s, st_s, (core, full), qs[core], [ks.at[k] for k in slots]) for core in cores]
 
     def own_main():
         got = km.at[RING, 0:256]
@@ -290,15 +297,15 @@
         for side in range(2):
             keep = HALF[1 - side]
             pltpu.make_async_copy(km.at[0, keep], km.at[RING + side, keep], old_sem.at[side]).wait()
-        absorb(main_jobs(0, (OTHER,)) + [
-            (acc_m, st_m, (OWN, HALF[side]), qm[OWN, HALF[side]], km.at[RING + side]) for side in range(2)
+        absorb(main_jobs(0, cores=(OTHER,)) + [
+            (acc_m, st_m, (OWN, HALF[side]), qm[OWN, HALF[side]], [km.at[RING + side]]) for side in range(2)
         ])
 
     def own_shared():
         pltpu.make_async_copy(ks.at[RING], ks.at[RING], new_recv.at[SHARED]).wait()
-        absorb(shared_jobs(0, (OTHER,)) + [
-            (acc_s, st_s, (OWN, HALF[0]), qs[OWN, HALF[0]], ks.at[RING]),
-            (acc_s, st_s, (OWN, HALF[1]), qs[OWN, HALF[1]], ks.at[0]),
+        absorb(shared_jobs(0, cores=(OTHER,)) + [
+            (acc_s, st_s, (OWN, HALF[0]), qs[OWN, HALF[0]], [ks.at[RING]]),
+            (acc_s, st_s, (OWN, HALF[1]), qs[OWN, HALF[1]], [ks.at[0]]),
         ])
 
     main_parts = [
@@ -372,20 +379,13 @@
                 obuf.at[rows(256 + zl * TOK, TOK)], outbuf.at[:, my_shared], out_recv
             ).start()
 
-    def lead(k, carry):
-        absorb(shared_jobs(k))
-        return carry
-
     def catch_up(i, carry):
         k = AHEAD + 1 + i
         take(SHARED, k + LEAD, AHEAD + LEAD + 1, EVEN + LEAD + 1)
         take(MAIN, k, AHEAD + 1, EVEN + 1)
 
-        def one(j, inner):
-            absorb(main_jobs(1 + 2 * i + j) + shared_jobs(1 + 2 * i + j + LEAD))
-            return inner
-
-        lax.fori_loop(0, 2, one, 0)
+        at = 1 + 2 * i
+        absorb(main_jobs(at, at + 1) + shared_jobs(at + LEAD, at + LEAD + 1))
         return carry
 
     def keep_up(k, carry):
@@ -399,14 +399,16 @@
         absorb(main_jobs(k))
         return carry
 
-    lax.fori_loop(1, LEAD + 1, lead, 0)
+    absorb(shared_jobs(*range(1, LEAD + 1)))
     lax.fori_loop(0, EVEN - AHEAD, catch_up, 0)
     lax.fori_loop(EVEN + 1, RING - LEAD, keep_up, 0)
     own_shared()
     for copy in shared_parts:
         copy.start()
-    lax.fori_loop(RING - LEAD, RING, trail, 0)
+    lax.fori_loop(RING - LEAD, RING - 1, trail, 0)
     own_main()
+    arrived(MAIN, RING - 1)
+    absorb(main_jobs(RING - 1))
     for copy in main_parts:
         copy.start()
     out_main()

time: 65.4 us -> 63.4 us (0.969)
  Pallas kernels: 62.8 us -> 60.6 us
    pallas_call x1, Pallas kernels: 62.8 us -> 60.6 us  [body(): pl.pallas_call(kernel, out_shape=jax.ShapeDtypeStruct(queries.shape, bf),...]
where the time goes in v4:
time: 63.4 us; the launch traced here: 62.8 us
  Pallas kernels  60.6 us (96%)
  local copies, waits for them, and re-layouts  1.54 us (2%)
  between operations  0.66 us (1%)
    pallas_call x1, Pallas kernels, body(): pl.pallas_call(kernel, out_shape=jax.ShapeDtypeStruct(queries.shape, bf),...  60.6 us
    unnamed x1, local copies, waits for them, and re-layouts  1.54 us

profile of v4, /device:TPU:1, one launch (start us, length us, event | category | flops | bytes accessed | tf_op | source)
XLA Modules:
  0.0 62.8 jit_solution(9896959254924340811)
XLA Ops:
  0.7 60.6 %shard_map.73 = bf16[16,3072]{1,0:T(8,128)(2,1)} custom-call(bf16[16,3072]{1,0:T(8,128)(2,1)} %q_in.1, bf16[16,3072]{1,0:T(8,128)(2,1)} %kn_in.1, bf16[16,3072]{1,0:T(8,128)(2,1)} %vn_in.1, bf16[16,3072]{1,0:T(8,128)(2,1)} %ko_in.1, bf16[16,3072]{1,0:T(8,128)(2,1)} %vo_in.1, f32[50,3072]{1,0:T(8,128)} %gate_in.1, s32[1]{0:T(128)S(6)} %copy.9.step_ref), custom_call_target="tpu_custom_call" | custom-call | tf_op jit(solution)/shard_map/pallas_call | solution.py:446
  61.2 1.5 %copy.10 = bf16[16,3072]{1,0:T(8,128)(2,1)} copy(bf16[16,3072]{1,0:T(8,128)(2,1)} %shard_map.73) | data formatting | bytes 196608
